TPU v7x, 32 devices: a whole 2x2x4 slice. The times are simulated.
32 devices in a mesh: dec: 8 (over z, x), ra: 4 (over y, core).
Axes of the slice: x: 2, y: 2, z: 4, core: 2. Of those that a mesh axis runs over, the one named last changes fastest.
Arguments:
- split_maps: bfloat16 [6, 2048, 1024], P(None, 'dec', 'ra'), may hold values from -40 to 40
- white_noise: bfloat16 [4096, 2048], P('dec', 'ra'), may hold values from -6 to 6
Outputs:
- noise_realization: float32 [2048, 1024], P('dec', 'ra')
All inputs are finite; a program needn't handle non-finite values.
Results may differ from a plain program's by a relative error of at most 0.0035.
The roundings to bfloat16 on the way count: a program that leaves them out, or rounds other values in their place, can miss the bound.
Values may be sent and summed in bfloat16 or wider, within the bound.
A program may use at most 64 MiB of HBM per device.

v0:
```python
import functools

import jax
import jax.numpy as jnp
import numpy as np
from jax import lax
from jax.experimental import pallas as pl
from jax.experimental.pallas import tpu as pltpu
from jax.sharding import PartitionSpec as P

SMOOTH = 4
MESH = pl.DeviceIdType.MESH
F32 = jnp.float32
BF16 = jnp.bfloat16
PAD = 16


def make_constants(length):
    half = length // 2
    indices = np.arange(length)
    angles = (indices[:, None] * indices[None, :] % length) * (2.0 * np.pi / length)
    cos_table, sin_table = np.cos(angles), np.sin(angles)
    packed = np.concatenate([cos_table[: half + 1], sin_table[1:half]], axis=0)
    profile = np.sin(np.pi * (indices + 0.5) / length) ** 2
    distance = np.abs(indices[:, None] - indices[None, :])
    near = (np.minimum(distance, length - distance) <= SMOOTH).astype(np.float64)
    mirrored = near[:, (-indices) % length]
    even = (near + mirrored)[: half + 1, :half]
    even[:, 0] = near[: half + 1, 0]
    odd = (near - mirrored)[:half, :half]
    odd[0, :] = 0.0
    odd[:, 0] = 0.0
    even_rows = np.zeros((half + PAD, half))
    even_rows[: half + 1] = even
    even_cols = np.zeros((half, half + 128))
    even_cols[:, : half + 1] = even.T
    edge = np.zeros((half + 128,))
    edge[: half + 1] = near[: half + 1, half]
    return dict(
        packed=packed, profile=profile, even_rows=even_rows, even_cols=even_cols, odd=odd,
        edge=edge, total=float(np.sum(profile**2) ** 2),
    )


def dot(left, right):
    return jnp.dot(left, right, preferred_element_type=F32)


def parts_of(values):
    high = values.astype(BF16)
    return high, (values - high.astype(F32)).astype(BF16)


def fine_left(matrix, values):
    high, low = parts_of(values)
    return dot(matrix, high) + dot(matrix, low)


def fine_right(values, matrix):
    high, low = parts_of(values)
    return dot(high, matrix) + dot(low, matrix)


def contrast(number, planes):
    if number < 3:
        return planes[2 * number] - planes[2 * number + 1]
    pair = [planes[2 * i] + planes[2 * i + 1] for i in range(3)]
    return pair[0] - pair[1] if number == 3 else pair[0] + pair[1] - 2.0 * pair[2]


WEIGHTS = (0.5, 0.5, 0.5, 0.25, 1.0 / 12.0)
PLANES = 5


def gains(squares, cross, even_rows, even_cols, odd, edge_rows, edge_cols, scale):
    half = cross.shape[0]
    rows = lax.broadcasted_iota(jnp.int32, (half, half), 0)
    cols = lax.broadcasted_iota(jnp.int32, (half, half), 1)
    a, b = squares[:half, :half], squares[:half, half:]
    d, e = squares[half:, :half], squares[half:, half:]
    inner_row, inner_col = rows > 0, cols > 0
    zero = jnp.zeros_like(a)
    e_col = jnp.where(inner_col, e, zero)
    top = a + jnp.where(inner_col, b, zero) + jnp.where(inner_row, d + e_col, zero)
    last_col = b + jnp.where(inner_row, e, zero)
    last_row = jnp.concatenate([(d + e_col)[:1], e[:1, :128]], axis=1)
    wide = jnp.concatenate([top, last_col[:, :128]], axis=1)
    once = fine_left(even_rows, wide) + edge_rows * last_row
    smooth = fine_right(once[:, :half], even_cols) + once[:, half : half + 1] * edge_cols
    twist = jnp.where(inner_row & inner_col, cross, zero)
    turned = fine_right(fine_left(odd, twist), odd)
    root = lambda values: jnp.sqrt(jnp.maximum(values * scale, 0.0))
    even = smooth[:half, :half]
    return (
        root(even + turned), root(even - turned),
        root(smooth[half : half + 1, :half]), root(smooth[:half, half : half + 1]),
        root(smooth[half : half + 1, half : half + 1]),
    )


def shaped(noise, plus, minus, last_row, last_col, corner):
    half = plus.shape[0]
    rows = lax.broadcasted_iota(jnp.int32, (half, half), 0)
    cols = lax.broadcasted_iota(jnp.int32, (half, half), 1)
    first_row, first_col = rows == 0, cols == 0
    either, both = first_row | first_col, first_row & first_col
    rounded = lambda values: values.astype(BF16).astype(F32)
    a, b = noise[:half, :half], noise[:half, half:]
    d, e = noise[half:, :half], noise[half:, half:]
    re_plus, re_minus = rounded(plus * (a - e)), rounded(minus * (a + e))
    im_plus, im_minus = rounded(plus * (b + d)), rounded(minus * (b - d))
    times = jnp.where(both, 1.0, 2.0)
    row_gain = jnp.where(first_row, last_row, plus)
    col_gain = jnp.where(first_col, last_col, plus)
    end_gain = jnp.where(both, corner, jnp.where(first_row, last_row, last_col))
    pick = lambda gain, block, inner: jnp.where(either, times * rounded(gain * block), 2.0 * inner)
    rest = lambda inner: jnp.where(either, 0.0, 2.0 * inner)
    joined = lambda z00, z01, z10, z11: jnp.concatenate(
        [jnp.concatenate([z00, z01], axis=1), jnp.concatenate([z10, z11], axis=1)], axis=0
    ).astype(BF16)
    first = joined(
        pick(plus, a, re_plus), pick(col_gain, b, im_plus),
        pick(row_gain, d, im_plus), pick(end_gain, e, -re_plus),
    )
    return first, joined(rest(re_minus), rest(im_minus), rest(-im_minus), rest(re_minus))


def kernel(
    n_dec, n_ra, scale,
    maps_hbm, noise_hbm, table_hbm, turned_hbm, rows_hbm, cols_hbm, odd_hbm,
    tall_hbm, wide_hbm, edge_rows_hbm, edge_cols_hbm,
    out_ref,
    maps, noise, table, turned, even_rows, even_cols, odd,
    tall_ref, wide_ref, edge_rows_ref, edge_cols_ref,
    ext, window, squares, cross, spectrum, real, strip_out, strip_in, row_out, row_in,
    local_sem, send_sem, recv_sem, fold_send, fold_recv,
):
    dec, ra = lax.axis_index("dec"), lax.axis_index("ra")
    length = noise.shape[0]
    core = length // 2
    margin = core // 2
    half = core
    low, mid, high = pl.ds(0, margin), pl.ds(margin, core), pl.ds(margin + core, margin)
    head, tail = pl.ds(margin, margin), pl.ds(core, margin)
    exists = {"up": dec > 0, "down": dec < n_dec - 1, "left": ra > 0, "right": ra < n_ra - 1}
    target = {
        "up": {"dec": dec - 1}, "down": {"dec": dec + 1},
        "left": {"ra": ra - 1}, "right": {"ra": ra + 1},
    }
    opposite = {"up": "down", "down": "up", "left": "right", "right": "left"}

    pairs = [
        pltpu.make_async_copy(maps_hbm.at[pl.ds(2 * i, 2)], maps.at[pl.ds(2 * i, 2)], local_sem.at[i])
        for i in range(3)
    ]
    loads = [
        pltpu.make_async_copy(source, place, local_sem.at[3 + number])
        for number, (source, place) in enumerate(
            [(tall_hbm, tall_ref), (wide_hbm, wide_ref), (noise_hbm, noise), (table_hbm, table),
             (turned_hbm, turned), (rows_hbm, even_rows), (cols_hbm, even_cols), (odd_hbm, odd),
             (edge_rows_hbm, edge_rows_ref), (edge_cols_hbm, edge_cols_ref)]
        )
    ]
    for load in pairs:
        load.start()

    barrier = pltpu.get_barrier_semaphore()
    for way in exists:
        @pl.when(exists[way])
        def _(way=way):
            pl.semaphore_signal(barrier, inc=1, device_id=target[way], device_id_type=MESH)
    inner = pl.ds(1, 2)
    moves = [
        ("up", head, 1, high, 1), ("down", tail, 1, low, 1),
        ("up", head, 2, high, 2), ("down", tail, 2, low, 2),
        ("left", mid, 1, mid, 3), ("right", mid, 2, mid, 0),
        ("left", high, 1, high, 3), ("left", low, 1, low, 3),
        ("right", high, 2, high, 0), ("right", low, 2, low, 0),
    ]

    def move(plane, number):
        way, rows, blocks, to_rows, to_blocks = moves[number]
        return pltpu.make_async_remote_copy(
            src_ref=ext.at[plane, blocks, rows, :],
            dst_ref=ext.at[plane, to_blocks, to_rows, :],
            send_sem=send_sem.at[plane, number],
            recv_sem=recv_sem.at[plane, number],
            device_id=target[way],
            device_id_type=MESH,
        )

    def start(plane, numbers):
        for number in numbers:
            @pl.when(exists[moves[number][0]])
            def _(number=number):
                move(plane, number).start()

    def wait_recv(plane, numbers):
        for number in numbers:
            @pl.when(exists[opposite[moves[number][0]]])
            def _(number=number):
                move(plane, number).wait_recv()

    def wait_send(plane, numbers):
        for number in numbers:
            @pl.when(exists[moves[number][0]])
            def _(number=number):
                move(plane, number).wait_send()

    for plane in range(PLANES):
        if plane < 3:
            pairs[plane].wait()
        used = range(6) if plane >= 3 else range(2 * plane, 2 * plane + 2)
        values = contrast(plane, {s: maps[s].astype(F32) for s in used}).astype(BF16)
        ext[plane, 1, mid, :] = values[:, :margin]
        ext[plane, 2, mid, :] = values[:, margin:]
        if plane == 0:
            pl.semaphore_wait(barrier, sum(here.astype(jnp.int32) for here in exists.values()))
        start(plane, (0, 1, 2, 3, 4, 5))

    for load in loads:
        load.start()
    whole = pl.ds(0, length)
    for way, rows, blocks in (
        ("up", low, inner), ("down", high, inner), ("left", whole, pl.ds(0, 1)), ("right", whole, pl.ds(3, 1)),
    ):
        @pl.when(jnp.logical_not(exists[way]))
        def _(rows=rows, blocks=blocks):
            ext[:, blocks, rows, :] = jnp.zeros((PLANES, blocks.size, rows.size, margin), BF16)

    for load in loads:
        load.wait()
    window[...] = tall_ref[...] * wide_ref[...]
    squares[...] = jnp.zeros_like(squares)
    cross[...] = jnp.zeros_like(cross)

    def transform(tile):
        return dot(dot(table[...], tile).astype(BF16), turned[...])

    spectrum[...] = transform(noise[...])

    def forward_corners(plane):
        for number in range(4):
            wait_recv(plane, (number,))
            start(plane, (6 + number,))

    def windowed(plane, rows, blocks):
        tile = jnp.concatenate([ext[plane, block, rows, :] for block in blocks], axis=1)
        shape = jnp.concatenate(
            [window[rows, block * margin : (block + 1) * margin] for block in blocks], axis=1
        )
        return (shape * tile.astype(F32)).astype(BF16)

    def gather_power(plane):
        wait_recv(plane, range(4, 10))
        add_power(plane, transform(windowed(plane, whole, range(4))))

    def gather_last(plane):
        halves = dot(table[...], windowed(plane, whole, (1, 2))).astype(BF16)
        spectrum_mid = dot(halves, turned[mid, :])
        wait_recv(plane, (4, 5))
        sides = dot(table[:, mid], windowed(plane, mid, (0, 3)))
        wait_recv(plane, range(6, 10))
        sides = sides + dot(table[:, low], windowed(plane, low, (0, 3)))
        sides = (sides + dot(table[:, high], windowed(plane, high, (0, 3)))).astype(BF16)
        add_power(
            plane,
            spectrum_mid + dot(sides[:, :margin], turned[low, :]) + dot(sides[:, margin:], turned[high, :]),
        )

    def add_power(plane, values):
        weight = jnp.where(
            plane < 3, WEIGHTS[0], jnp.where(plane == 3, WEIGHTS[3], WEIGHTS[4])
        ).astype(F32)
        squares[...] += values * values * weight
        a, b = values[:half, :half], values[:half, half:]
        d, e = values[half:, :half], values[half:, half:]
        cross[...] += (b * d - a * e) * (2.0 * weight)

    forward_corners(0)

    def step(plane, carry):
        forward_corners(plane)
        gather_power(plane - 1)
        return carry

    lax.fori_loop(1, PLANES, step, 0)
    gather_last(PLANES - 1)

    filters = gains(
        squares[...], cross[...], even_rows[...], even_cols[...], odd[...],
        edge_rows_ref[...], edge_cols_ref[...], scale,
    )
    mixed, mirrored = shaped(spectrum[...], *filters)

    def inverse(rows):
        return (dot(turned[rows, :], mixed) + dot(turned[rows, :], mirrored)).astype(BF16)

    def synthesize(part, rows, cols):
        real[rows, cols] = window[rows, cols] * dot(part, table[:, cols])

    def strip(side, rows, number):
        return pltpu.make_async_remote_copy(
            src_ref=strip_out.at[side, rows, :],
            dst_ref=strip_in.at[side, rows, :],
            send_sem=fold_send.at[side, number],
            recv_sem=fold_recv.at[side, number],
            device_id=target[("left", "right")[side]],
            device_id_type=MESH,
        )

    def band(side):
        return pltpu.make_async_remote_copy(
            src_ref=row_out.at[side],
            dst_ref=row_in.at[side],
            send_sem=fold_send.at[side, 3],
            recv_sem=fold_recv.at[side, 3],
            device_id=target[("up", "down")[side]],
            device_id_type=MESH,
        )

    pieces = ((low, 0), (high, 1), (mid, 2))
    ways = ("left", "right")
    def send_strips(part, rows, number):
        for side, cols in enumerate((low, high)):
            values = window[rows, cols] * dot(part, table[:, cols])
            strip_out[side, rows, :] = values.astype(BF16)
            @pl.when(exists[ways[side]])
            def _(side=side, rows=rows, number=number):
                strip(side, rows, number).start()

    outer = [inverse(rows) for rows, number in pieces[:2]]
    for part, (rows, number) in zip(outer, pieces):
        send_strips(part, rows, number)
    middle = inverse(mid)
    send_strips(middle, *pieces[2])
    for part, (rows, number) in zip(outer + [middle], pieces):
        synthesize(part, rows, mid)

    def fold_columns(rows, number):
        for side, cols in ((1, head), (0, tail)):
            @pl.when(exists[opposite[ways[side]]])
            def _(side=side, cols=cols):
                strip(side, rows, number).wait_recv()
                real[rows, cols] += strip_in[side, rows, :].astype(F32)

    for side, (rows, number) in enumerate(pieces[:2]):
        fold_columns(rows, number)
        row_out[side] = real[rows, mid].astype(BF16)
        @pl.when(exists[("up", "down")[side]])
        def _(side=side):
            band(side).start()
    fold_columns(*pieces[2])
    for side, rows in ((1, head), (0, tail)):
        @pl.when(exists[("down", "up")[side]])
        def _(side=side, rows=rows):
            band(side).wait_recv()
            real[rows, mid] += row_in[side].astype(F32)
    out_ref[...] = real[mid, mid]

    def drain(plane, carry):
        wait_send(plane, range(10))
        return carry

    lax.fori_loop(0, PLANES, drain, 0)
    for side in range(2):
        @pl.when(exists[ways[side]])
        def _(side=side):
            for rows, number in pieces:
                strip(side, rows, number).wait_send()

        @pl.when(exists[("up", "down")[side]])
        def _(side=side):
            band(side).wait_send()


def shards(n_dec, n_ra, constants, split_maps, white_noise):
    splits, core = split_maps.shape[0], split_maps.shape[1]
    length, half, margin = 2 * core, core, core // 2
    as_bf16 = lambda values: jnp.asarray(np.asarray(values, np.float32).astype(jnp.bfloat16))
    as_f32 = lambda values: jnp.asarray(np.asarray(values, np.float32))
    packed = as_bf16(constants["packed"])
    turned = as_bf16(constants["packed"].T)
    edge = constants["edge"]
    scale = 1.0 / ((splits - 1) * constants["total"] * (2 * SMOOTH + 1) ** 2)
    in_vmem = pl.BlockSpec(memory_space=pltpu.VMEM)
    in_hbm = pl.BlockSpec(memory_space=pl.ANY)
    result = pl.pallas_call(
        functools.partial(kernel, n_dec, n_ra, scale),
        out_shape=jax.ShapeDtypeStruct((core, core), F32),
        in_specs=[in_hbm] * 11,
        out_specs=in_vmem,
        scratch_shapes=[
            pltpu.VMEM((splits, core, core), BF16),
            pltpu.VMEM((length, length), BF16),
            pltpu.VMEM((length, length), BF16),
            pltpu.VMEM((length, length), BF16),
            pltpu.VMEM((half + PAD, half), BF16),
            pltpu.VMEM((half, half + 128), BF16),
            pltpu.VMEM((half, half), BF16),
            pltpu.VMEM((length, 1), F32),
            pltpu.VMEM((1, length), F32),
            pltpu.VMEM((half + PAD, 1), F32),
            pltpu.VMEM((1, half + 128), F32),
            pltpu.VMEM((PLANES, 4, length, margin), BF16),
            pltpu.VMEM((length, length), F32),
            pltpu.VMEM((length, length), F32),
            pltpu.VMEM((half, half), F32),
            pltpu.VMEM((length, length), F32),
            pltpu.VMEM((length, length), F32),
            pltpu.VMEM((2, length, margin), BF16),
            pltpu.VMEM((2, length, margin), BF16),
            pltpu.VMEM((2, margin, core), BF16),
            pltpu.VMEM((2, margin, core), BF16),
            pltpu.SemaphoreType.DMA((13,)),
            pltpu.SemaphoreType.DMA((PLANES, 10)),
            pltpu.SemaphoreType.DMA((PLANES, 10)),
            pltpu.SemaphoreType.DMA((2, 4)),
            pltpu.SemaphoreType.DMA((2, 4)),
        ],
        compiler_params=pltpu.CompilerParams(
            collective_id=0, has_side_effects=True, vmem_limit_bytes=56 << 20
        ),
    )(
        split_maps, white_noise, packed, turned,
        as_bf16(constants["even_rows"]), as_bf16(constants["even_cols"]), as_bf16(constants["odd"]),
        as_f32(constants["profile"][:, None]), as_f32(constants["profile"][None, :]),
        as_f32(edge[: half + PAD, None]), as_f32(edge[None, :]),
    )
    return result * (1.0 / (length * length))


def solution(mesh):
    n_dec, n_ra = mesh.shape["dec"], mesh.shape["ra"]

    def body(split_maps, white_noise):
        constants = make_constants(2 * split_maps.shape[1])
        return shards(n_dec, n_ra, constants, split_maps, white_noise)

    placed = (P(None, "dec", "ra"), P("dec", "ra"))
    return jax.shard_map(
        body, mesh=mesh, in_specs=placed, out_specs=P("dec", "ra"), check_vma=False
    )
```

profile of v0, /device:TPU:0, one launch (start us, length us, event | category | flops | bytes accessed | tf_op | source)
XLA Modules:
  0.0 34.5 jit_solution(4258268274024497542)
XLA Ops:
  0.0 32.9 %shard_map.109 = f32[256,256]{1,0:T(8,128)} custom-call(bf16[6,256,256]{2,1,0:T(8,128)(2,1)} %maps_hbm.1, bf16[512,512]{1,0:T(8,128)(2,1)} %noise_hbm.1, bf16[512,512]{1,0:T(8,128)(2,1)} %constant.20.clone.table_hbm, bf16[512,512]{1,0:T(8,128)(2,1)} %constant.21.clone.turned_hbm, bf16[272,256]{1,0:T(8,128)(2,1)} %constant.22.clone.rows_hbm, ...), custom_call_target="tpu_custom_call" | custom-call | tf_op jit(solution)/shard_map/pallas_call | solution.py:388
  32.9 1.7 %broadcast_multiply_fusion = f32[256,256]{1,0:T(8,128)} fusion(f32[256,256]{1,0:T(8,128)} %shard_map.109), kind=kLoop, calls=%fused_computation | loop fusion | flops 65536 | bytes 524288 | tf_op jit(solution)/shard_map/mul | solution.py:430
where the time goes:
time: 35.1 us; the launch traced here: 34.5 us
  Pallas kernels  32.9 us (94%)
  other arithmetic  1.67 us (5%)
    pallas_call x1, Pallas kernels, shards(): pl.pallas_call(functools.partial(kernel, n_dec, n_ra, scale), out_shape=j...  32.9 us
    mul x1, other arithmetic, shards(): return result * (1.0 / (length * length))  1.67 us

commit v1 on v0

--- a/solution.py
+++ b/solution.py
@@ -387,7 +387,7 @@
     in_hbm = pl.BlockSpec(memory_space=pl.ANY)
     result = pl.pallas_call(
         functools.partial(kernel, n_dec, n_ra, scale),
-        out_shape=jax.ShapeDtypeStruct((core, core), F32),
+        out_shape=pltpu.VMEM((core, core), F32),
         in_specs=[in_hbm] * 11,
         out_specs=in_vmem,
         scratch_shapes=[

time: 35.1 us -> 33.4 us (0.952)
  other arithmetic: 1.67 us -> 0.72 us
  Pallas kernels: 32.9 us -> 32.2 us
    mul x1, other arithmetic: 1.67 us -> 0.72 us  [shards(): return result * (1.0 / (length * length))]
    pallas_call x1, Pallas kernels: 32.9 us -> 32.2 us  [shards(): pl.pallas_call(functools.partial(kernel, n_dec, n_ra, scale), out_shape=p...]
where the time goes in v1:
time: 33.4 us; the launch traced here: 32.9 us
  Pallas kernels  32.2 us (96%)
  other arithmetic  0.72 us (2%)
    pallas_call x1, Pallas kernels, shards(): pl.pallas_call(functools.partial(kernel, n_dec, n_ra, scale), out_shape=p...  32.2 us
    mul x1, other arithmetic, shards(): return result * (1.0 / (length * length))  0.72 us

profile of v1, /device:TPU:0, one launch (start us, length us, event | category | flops | bytes accessed | tf_op | source)
XLA Modules:
  0.0 32.9 jit_solution(3976525539112425457)
XLA Ops:
  0.0 32.2 %shard_map.109 = f32[256,256]{1,0:T(8,128)S(1)} custom-call(bf16[6,256,256]{2,1,0:T(8,128)(2,1)} %maps_hbm.1, bf16[512,512]{1,0:T(8,128)(2,1)} %noise_hbm.1, bf16[512,512]{1,0:T(8,128)(2,1)} %constant.20.clone.table_hbm, bf16[512,512]{1,0:T(8,128)(2,1)} %constant.21.clone.turned_hbm, bf16[272,256]{1,0:T(8,128)(2,1)} %constant.22.clone.rows_hbm, ...), custom_call_target="tpu_custom_call" | custom-call | tf_op jit(solution)/shard_map/pallas_call | solution.py:388
  32.2 0.7 %broadcast_multiply_fusion = f32[256,256]{1,0:T(8,128)} fusion(f32[256,256]{1,0:T(8,128)S(1)} %shard_map.109), kind=kLoop, calls=%fused_computation | loop fusion | flops 65536 | bytes 524288 | tf_op jit(solution)/shard_map/mul | solution.py:430

commit v2 on v1

v2 whole, which is shorter than its diff:
```python
import functools

import jax
import jax.numpy as jnp
import numpy as np
from jax import lax
from jax.experimental import pallas as pl
from jax.experimental.pallas import tpu as pltpu
from jax.sharding import PartitionSpec as P

SMOOTH = 4
MESH = pl.DeviceIdType.MESH
F32 = jnp.float32
BF16 = jnp.bfloat16
PAD = 16


def make_constants(length):
    half = length // 2
    indices = np.arange(length)
    angles = (indices[:, None] * indices[None, :] % length) * (2.0 * np.pi / length)
    cos_table, sin_table = np.cos(angles), np.sin(angles)
    packed = np.concatenate([cos_table[: half + 1], sin_table[1:half]], axis=0)
    profile = np.sin(np.pi * (indices + 0.5) / length) ** 2

    def near(left, right):
        distance = np.abs(left[:, None] - right[None, :]) % length
        return (np.minimum(distance, length - distance) <= SMOOTH).astype(np.float64)

    signed = np.concatenate([np.arange(half + 1), -np.arange(1, half)])
    kept = np.arange(half + PAD)
    smooth_rows = near(kept, np.arange(half)) * (kept <= half)[:, None]
    first = np.arange(PAD)
    fold_first = near(first, -first) * (first > 0)[None, :]
    last = half - PAD + np.arange(2 * PAD)
    fold_last = np.zeros((2 * PAD, 2 * PAD))
    fold_last[:, :PAD] = near(last, -last[:PAD])
    fold_last[:, PAD] = near(last, np.array([half]))[:, 0]
    fold_last[last > half] = 0.0
    return dict(
        packed=packed, profile=profile, smooth_cols=near(signed, signed), smooth_rows=smooth_rows,
        fold_first=fold_first, fold_last=fold_last, total=float(np.sum(profile**2) ** 2),
    )


def dot(left, right):
    return jnp.dot(left, right, preferred_element_type=F32)


def parts_of(values):
    high = values.astype(BF16)
    return high, (values - high.astype(F32)).astype(BF16)


def fine_left(matrix, values):
    high, low = parts_of(values)
    return dot(matrix, high) + dot(matrix, low)


def fine_right(values, matrix):
    high, low = parts_of(values)
    return dot(high, matrix) + dot(low, matrix)


def contrast(number, planes):
    if number < 3:
        return planes[2 * number] - planes[2 * number + 1]
    pair = [planes[2 * i] + planes[2 * i + 1] for i in range(3)]
    if number == 3:
        return (pair[0] - pair[1]) * 0.5**0.5
    return (pair[0] + pair[1] - 2.0 * pair[2]) * (1.0 / 6.0) ** 0.5


WEIGHT = 0.5
PLANES = 5


def first_lane(rows, cols):
    return lax.broadcasted_iota(jnp.int32, (rows, cols), 1) == 0


def first_row(rows, cols):
    return lax.broadcasted_iota(jnp.int32, (rows, cols), 0) == 0


def edge_line(squares):
    half = squares.shape[1] // 2
    lane = first_lane(squares.shape[0], half)
    left, right = squares[:, :half], squares[:, half:]
    both = left + right
    return jnp.concatenate([jnp.where(lane, left, both), jnp.where(lane, right, both)], axis=1)


def mirrored_cols(values):
    half = values.shape[1] // 2
    lane = first_lane(values.shape[0], half)
    left, right = values[:, :half], values[:, half:]
    return jnp.concatenate([jnp.where(lane, left, right), jnp.where(lane, right, left)], axis=1)


def gains(power, edge_rows, edge_cols, smooth_rows, smooth_cols, fold_first, fold_last):
    half = power.shape[0]
    lane = first_lane(half, 128)
    whole = jnp.concatenate(
        [
            jnp.where(lane, edge_cols[:, :128], power[:, :128]), power[:, 128:half],
            jnp.where(lane, edge_cols[:, 128:], power[:, half : half + 128]), power[:, half + 128 :],
        ],
        axis=1,
    )
    top = jnp.where(first_row(8, 2 * half), edge_line(edge_rows[:8]), whole[:8])
    nyquist = edge_line(edge_rows[8:])
    whole = jnp.concatenate([top, whole[8:], nyquist, jnp.zeros_like(nyquist)], axis=0)
    once = fine_right(whole, smooth_cols)
    smooth = fine_left(smooth_rows, once[:half])
    start = smooth[:PAD] + fine_left(fold_first, mirrored_cols(once[:PAD]))
    tail = jnp.concatenate([mirrored_cols(once[half - PAD : half]), once[half:]], axis=0)
    end = smooth[half - PAD :] + fine_left(fold_last, tail)
    return jnp.sqrt(jnp.concatenate([start, smooth[PAD : half - PAD], end[: PAD + 8]], axis=0))


def combine(noise, factor, sums, edge, last):
    half = noise.shape[0] // 2
    values = noise * factor
    a, b = values[:half, :half], values[:half, half:]
    d, e = values[half:, :half], values[half:, half:]
    rows, lane = first_row(half, half), first_lane(half, half)
    either, both = rows | lane, rows & lane
    zero = jnp.zeros_like(a)
    sums[0] = jnp.where(both, a, 2.0 * (a - jnp.where(either, zero, e)))
    sums[1] = 2.0 * (jnp.where(lane, zero, b) + jnp.where(rows, zero, d))
    sums[2] = jnp.where(either, zero, 2.0 * (a + e))
    sums[3] = jnp.where(either, zero, 2.0 * (b - d))
    edge[0] = jnp.where(both, b, 2.0 * b)[:, :128]
    edge[1] = (2.0 * e)[:, :128]
    bottom = values[half : half + 8]
    single = first_lane(8, half)
    single = jnp.concatenate([single, single], axis=1)
    last[...] = jnp.where(single, bottom, 2.0 * bottom)


def shaped(gain, sums, edge, last):
    half = sums.shape[1]
    plus, minus = gain[:half, :half], gain[:half, half:]
    lane = first_lane(half, 128)
    row = first_row(8, half)
    line = gain[half : half + 8] * last[...]

    def with_lane(values, fixed):
        return jnp.concatenate([jnp.where(lane, minus[:, :128] * fixed, values[:, :128]), values[:, 128:]], axis=1)

    def with_row(values, fixed):
        return jnp.concatenate([jnp.where(row, fixed, values[:8]), values[8:]], axis=0)

    real_plus, imag_plus = plus * sums[0], plus * sums[1]
    real_minus, imag_minus = (minus * sums[2]).astype(BF16), (minus * sums[3]).astype(BF16)
    return (
        jnp.concatenate([real_plus.astype(BF16), with_lane(imag_plus, edge[0]).astype(BF16)], axis=1),
        jnp.concatenate(
            [
                with_row(imag_plus, line[:, :half]).astype(BF16),
                with_row(with_lane(-real_plus, edge[1]), line[:, half:]).astype(BF16),
            ],
            axis=1,
        ),
        jnp.concatenate([real_minus, imag_minus], axis=1),
        jnp.concatenate([-imag_minus, real_minus], axis=1),
    )


def kernel(
    n_dec, n_ra, factor,
    maps_hbm, noise_hbm, table_hbm, turned_hbm, rows_hbm, cols_hbm, first_hbm, last_hbm,
    tall_hbm, wide_hbm,
    out_ref,
    maps, noise, table, turned, smooth_rows, smooth_cols, fold_first, fold_last,
    tall_ref, wide_ref,
    ext, window, power, edge_rows, edge_cols, spectrum, sums, edge, last, real,
    strip_out, strip_in, row_out, row_in,
    local_sem, send_sem, recv_sem, fold_send, fold_recv,
):
    dec, ra = lax.axis_index("dec"), lax.axis_index("ra")
    length = noise.shape[0]
    core = length // 2
    margin = core // 2
    half = core
    low, mid, high = pl.ds(0, margin), pl.ds(margin, core), pl.ds(margin + core, margin)
    head, tail = pl.ds(margin, margin), pl.ds(core, margin)
    exists = {"up": dec > 0, "down": dec < n_dec - 1, "left": ra > 0, "right": ra < n_ra - 1}
    target = {
        "up": {"dec": dec - 1}, "down": {"dec": dec + 1},
        "left": {"ra": ra - 1}, "right": {"ra": ra + 1},
    }
    opposite = {"up": "down", "down": "up", "left": "right", "right": "left"}

    pairs = [
        pltpu.make_async_copy(maps_hbm.at[pl.ds(2 * i, 2)], maps.at[pl.ds(2 * i, 2)], local_sem.at[i])
        for i in range(3)
    ]
    loads = [
        pltpu.make_async_copy(source, place, local_sem.at[3 + number])
        for number, (source, place) in enumerate(
            [(tall_hbm, tall_ref), (wide_hbm, wide_ref), (noise_hbm, noise), (table_hbm, table),
             (turned_hbm, turned), (rows_hbm, smooth_rows), (cols_hbm, smooth_cols),
             (first_hbm, fold_first), (last_hbm, fold_last)]
        )
    ]
    for load in pairs:
        load.start()

    barrier = pltpu.get_barrier_semaphore()
    for way in exists:
        @pl.when(exists[way])
        def _(way=way):
            pl.semaphore_signal(barrier, inc=1, device_id=target[way], device_id_type=MESH)
    inner = pl.ds(1, 2)
    moves = [
        ("up", head, 1, high, 1), ("down", tail, 1, low, 1),
        ("up", head, 2, high, 2), ("down", tail, 2, low, 2),
        ("left", mid, 1, mid, 3), ("right", mid, 2, mid, 0),
        ("left", high, 1, high, 3), ("left", low, 1, low, 3),
        ("right", high, 2, high, 0), ("right", low, 2, low, 0),
    ]

    def move(plane, number):
        way, rows, blocks, to_rows, to_blocks = moves[number]
        return pltpu.make_async_remote_copy(
            src_ref=ext.at[plane, blocks, rows, :],
            dst_ref=ext.at[plane, to_blocks, to_rows, :],
            send_sem=send_sem.at[plane, number],
            recv_sem=recv_sem.at[plane, number],
            device_id=target[way],
            device_id_type=MESH,
        )

    def start(plane, numbers):
        for number in numbers:
            @pl.when(exists[moves[number][0]])
            def _(number=number):
                move(plane, number).start()

    def wait_recv(plane, numbers):
        for number in numbers:
            @pl.when(exists[opposite[moves[number][0]]])
            def _(number=number):
                move(plane, number).wait_recv()

    def wait_send(plane, numbers):
        for number in numbers:
            @pl.when(exists[moves[number][0]])
            def _(number=number):
                move(plane, number).wait_send()

    for plane in range(PLANES):
        if plane < 3:
            pairs[plane].wait()
        used = range(6) if plane >= 3 else range(2 * plane, 2 * plane + 2)
        values = contrast(plane, {s: maps[s].astype(F32) for s in used}).astype(BF16)
        ext[plane, 1, mid, :] = values[:, :margin]
        ext[plane, 2, mid, :] = values[:, margin:]
        if plane == 0:
            pl.semaphore_wait(barrier, sum(here.astype(jnp.int32) for here in exists.values()))
        start(plane, (0, 3, 2, 1, 4, 5))

    for load in loads:
        load.start()
    whole = pl.ds(0, length)
    for way, rows, blocks in (
        ("up", low, inner), ("down", high, inner), ("left", whole, pl.ds(0, 1)), ("right", whole, pl.ds(3, 1)),
    ):
        @pl.when(jnp.logical_not(exists[way]))
        def _(rows=rows, blocks=blocks):
            ext[:, blocks, rows, :] = jnp.zeros((PLANES, blocks.size, rows.size, margin), BF16)

    for load in loads:
        load.wait()
    window[...] = tall_ref[...] * wide_ref[...]
    for total in (power, edge_rows, edge_cols):
        total[...] = jnp.zeros_like(total)

    def transform(tile):
        return dot(dot(table[...], tile).astype(BF16), turned[...])

    combine(transform(noise[...]), factor, sums, edge, last)

    def forward_corners(plane):
        for number in (0, 3, 2, 1):
            wait_recv(plane, (number,))
            start(plane, (6 + number,))

    def windowed(plane, rows, blocks):
        tile = jnp.concatenate([ext[plane, block, rows, :] for block in blocks], axis=1)
        shape = jnp.concatenate(
            [window[rows, block * margin : (block + 1) * margin] for block in blocks], axis=1
        )
        return (shape * tile.astype(F32)).astype(BF16)

    def gather_power(plane):
        wait_recv(plane, range(4, 10))
        add_power(transform(windowed(plane, whole, range(4))))

    def outer_rows(values):
        return jnp.concatenate([values(low), values(high)], axis=0)

    def gather_last(plane):
        halves = dot(table[...], windowed(plane, whole, (1, 2))).astype(BF16)
        spectrum[...] = dot(halves, turned[mid, :])
        wait_recv(plane, (4, 5))
        sides = dot(table[:, mid], windowed(plane, mid, (0, 3)))
        wait_recv(plane, range(6, 10))
        corners = outer_rows(lambda rows: windowed(plane, rows, (0, 3)))
        outer_table = jnp.concatenate([table[:, low], table[:, high]], axis=1)
        sides = (sides + dot(outer_table, corners)).astype(BF16)
        add_power(spectrum[...] + dot(sides, outer_rows(lambda rows: turned[rows, :])))

    def add_power(values):
        a, b = values[:half, :half], values[:half, half:]
        d, e = values[half:, :half], values[half:, half:]
        square = lambda part: part * part
        power[:, :half] += square(a - e) + square(b + d)
        power[:, half:] += square(a + e) + square(b - d)
        edge_rows[:8] += square(values[:8])
        edge_rows[8:] += square(values[half : half + 8])
        edge_cols[:, :128] += square(a[:, :128]) + square(d[:, :128])
        edge_cols[:, 128:] += square(b[:, :128]) + square(e[:, :128])

    forward_corners(0)
    forward_corners(1)

    def step(plane, carry):
        forward_corners(plane)
        gather_power(plane - 2)
        return carry

    lax.fori_loop(2, PLANES, step, 0)
    gather_power(PLANES - 2)
    gather_last(PLANES - 1)

    gain = gains(
        power[...], edge_rows[...], edge_cols[...], smooth_rows[...], smooth_cols[...],
        fold_first[...], fold_last[...],
    )
    mixed = jnp.concatenate(shaped(gain, sums, edge, last), axis=0)

    def inverse(rows):
        return dot(jnp.concatenate([rows, rows], axis=1), mixed).astype(BF16)

    def synthesize(part, rows, cols):
        real[rows, cols] = window[rows, cols] * dot(part, table[:, cols])

    def strip(side, rows, number):
        return pltpu.make_async_remote_copy(
            src_ref=strip_out.at[side, rows, :],
            dst_ref=strip_in.at[side, rows, :],
            send_sem=fold_send.at[side, number],
            recv_sem=fold_recv.at[side, number],
            device_id=target[("left", "right")[side]],
            device_id_type=MESH,
        )

    def band(side):
        return pltpu.make_async_remote_copy(
            src_ref=row_out.at[side],
            dst_ref=row_in.at[side],
            send_sem=fold_send.at[side, 3],
            recv_sem=fold_recv.at[side, 3],
            device_id=target[("up", "down")[side]],
            device_id_type=MESH,
        )

    pieces = ((low, 0), (high, 1), (mid, 2))
    ways = ("left", "right")
    side_table = jnp.concatenate([table[:, low], table[:, high]], axis=1)

    def send_strips(part, numbers):
        values = dot(part, side_table)
        start = 0
        for number in numbers:
            rows = pieces[number][0]
            for side, cols in enumerate((low, high)):
                block = values[start : start + rows.size, side * margin : (side + 1) * margin]
                strip_out[side, rows, :] = (window[rows, cols] * block).astype(BF16)
                @pl.when(exists[ways[side]])
                def _(side=side, rows=rows, number=number):
                    strip(side, rows, number).start()
            start += rows.size

    outer = inverse(outer_rows(lambda rows: turned[rows, :]))
    send_strips(outer, (0, 1))
    middle = inverse(turned[mid, :])
    send_strips(middle, (2,))
    for part, (rows, number) in zip((outer[:margin], outer[margin:], middle), pieces):
        synthesize(part, rows, mid)

    def drain(plane, carry):
        wait_send(plane, range(10))
        return carry

    lax.fori_loop(0, PLANES, drain, 0)

    def fold_columns(rows, number):
        for side, cols in ((1, head), (0, tail)):
            @pl.when(exists[opposite[ways[side]]])
            def _(side=side, cols=cols):
                strip(side, rows, number).wait_recv()
                real[rows, cols] += strip_in[side, rows, :].astype(F32)

    for side, (rows, number) in enumerate(pieces[:2]):
        fold_columns(rows, number)
        row_out[side] = real[rows, mid].astype(BF16)
        @pl.when(exists[("up", "down")[side]])
        def _(side=side):
            band(side).start()
    fold_columns(*pieces[2])
    for side, rows in ((1, head), (0, tail)):
        @pl.when(exists[("down", "up")[side]])
        def _(side=side, rows=rows):
            band(side).wait_recv()
            real[rows, mid] += row_in[side].astype(F32)
    out_ref[...] = real[mid, mid]

    for side in range(2):
        @pl.when(exists[ways[side]])
        def _(side=side):
            for rows, number in pieces:
                strip(side, rows, number).wait_send()

        @pl.when(exists[("up", "down")[side]])
        def _(side=side):
            band(side).wait_send()


def shards(n_dec, n_ra, constants, split_maps, white_noise):
    splits, core = split_maps.shape[0], split_maps.shape[1]
    length, half, margin = 2 * core, core, core // 2
    as_bf16 = lambda values: jnp.asarray(np.asarray(values, np.float32).astype(jnp.bfloat16))
    as_f32 = lambda values: jnp.asarray(np.asarray(values, np.float32))
    packed = as_bf16(constants["packed"])
    turned = as_bf16(constants["packed"].T)
    scale = WEIGHT / ((splits - 1) * constants["total"] * (2 * SMOOTH + 1) ** 2)
    in_vmem = pl.BlockSpec(memory_space=pltpu.VMEM)
    in_hbm = pl.BlockSpec(memory_space=pl.ANY)
    result = pl.pallas_call(
        functools.partial(kernel, n_dec, n_ra, scale**0.5),
        out_shape=pltpu.VMEM((core, core), F32),
        in_specs=[in_hbm] * 10,
        out_specs=in_vmem,
        scratch_shapes=[
            pltpu.VMEM((splits, core, core), BF16),
            pltpu.VMEM((length, length), BF16),
            pltpu.VMEM((length, length), BF16),
            pltpu.VMEM((length, length), BF16),
            pltpu.VMEM((half + PAD, half), BF16),
            pltpu.VMEM((length, length), BF16),
            pltpu.VMEM((PAD, PAD), BF16),
            pltpu.VMEM((2 * PAD, 2 * PAD), BF16),
            pltpu.VMEM((length, 1), F32),
            pltpu.VMEM((1, length), F32),
            pltpu.VMEM((PLANES, 4, length, margin), BF16),
            pltpu.VMEM((length, length), F32),
            pltpu.VMEM((half, length), F32),
            pltpu.VMEM((PAD, length), F32),
            pltpu.VMEM((half, 256), F32),
            pltpu.VMEM((length, length), F32),
            pltpu.VMEM((4, half, half), F32),
            pltpu.VMEM((2, half, 128), F32),
            pltpu.VMEM((8, length), F32),
            pltpu.VMEM((length, length), F32),
            pltpu.VMEM((2, length, margin), BF16),
            pltpu.VMEM((2, length, margin), BF16),
            pltpu.VMEM((2, margin, core), BF16),
            pltpu.VMEM((2, margin, core), BF16),
            pltpu.SemaphoreType.DMA((13,)),
            pltpu.SemaphoreType.DMA((PLANES, 10)),
            pltpu.SemaphoreType.DMA((PLANES, 10)),
            pltpu.SemaphoreType.DMA((2, 4)),
            pltpu.SemaphoreType.DMA((2, 4)),
        ],
        compiler_params=pltpu.CompilerParams(
            collective_id=0, has_side_effects=True, vmem_limit_bytes=56 << 20
        ),
    )(
        split_maps, white_noise, packed, turned,
        as_bf16(constants["smooth_rows"]), as_bf16(constants["smooth_cols"]),
        as_bf16(constants["fold_first"]), as_bf16(constants["fold_last"]),
        as_f32(constants["profile"][:, None]), as_f32(constants["profile"][None, :]),
    )
    return result * (1.0 / (length * length))


def solution(mesh):
    n_dec, n_ra = mesh.shape["dec"], mesh.shape["ra"]

    def body(split_maps, white_noise):
        constants = make_constants(2 * split_maps.shape[1])
        return shards(n_dec, n_ra, constants, split_maps, white_noise)

    placed = (P(None, "dec", "ra"), P("dec", "ra"))
    return jax.shard_map(
        body, mesh=mesh, in_specs=placed, out_specs=P("dec", "ra"), check_vma=False
    )
```

time: 33.4 us -> 31.1 us (0.931)
  Pallas kernels: 32.2 us -> 29.8 us
    pallas_call x1, Pallas kernels: 32.2 us -> 29.8 us  [shards(): pl.pallas_call(functools.partial(kernel, n_dec, n_ra, scale ** 0.5), out_...]
where the time goes in v2:
time: 31.1 us; the launch traced here: 30.6 us
  Pallas kernels  29.8 us (96%)
  other arithmetic  0.72 us (2%)
    pallas_call x1, Pallas kernels, shards(): pl.pallas_call(functools.partial(kernel, n_dec, n_ra, scale ** 0.5), out_...  29.8 us
    mul x1, other arithmetic, shards(): return result * (1.0 / (length * length))  0.72 us

profile of v2, /device:TPU:0, one launch (start us, length us, event | category | flops | bytes accessed | tf_op | source)
XLA Modules:
  0.0 30.6 jit_solution(10514137504995464673)
XLA Ops:
  0.0 29.8 %shard_map.100 = f32[256,256]{1,0:T(8,128)S(1)} custom-call(bf16[6,256,256]{2,1,0:T(8,128)(2,1)} %maps_hbm.1, bf16[512,512]{1,0:T(8,128)(2,1)} %noise_hbm.1, bf16[512,512]{1,0:T(8,128)(2,1)} %constant.18.clone.table_hbm, bf16[512,512]{1,0:T(8,128)(2,1)} %constant.19.clone.turned_hbm, bf16[272,256]{1,0:T(8,128)(2,1)} %constant.20.clone.rows_hbm, ...), custom_call_target="tpu_custom_call" | custom-call | tf_op jit(solution)/shard_map/pallas_call | solution.py:443
  29.8 0.7 %broadcast_multiply_fusion = f32[256,256]{1,0:T(8,128)} fusion(f32[256,256]{1,0:T(8,128)S(1)} %shard_map.100), kind=kLoop, calls=%fused_computation | loop fusion | flops 65536 | bytes 524288 | tf_op jit(solution)/shard_map/mul | solution.py:488

commit v3 on v2

--- a/solution.py
+++ b/solution.py
@@ -176,7 +176,7 @@
     maps, noise, table, turned, smooth_rows, smooth_cols, fold_first, fold_last,
     tall_ref, wide_ref,
     ext, window, power, edge_rows, edge_cols, spectrum, sums, edge, last, real,
-    strip_out, strip_in, row_out, row_in,
+    strip_out, strip_in, row_out, row_in, corner_in,
     local_sem, send_sem, recv_sem, fold_send, fold_recv,
 ):
     dec, ra = lax.axis_index("dec"), lax.axis_index("ra")
@@ -345,9 +345,6 @@
     def inverse(rows):
         return dot(jnp.concatenate([rows, rows], axis=1), mixed).astype(BF16)
 
-    def synthesize(part, rows, cols):
-        real[rows, cols] = window[rows, cols] * dot(part, table[:, cols])
-
     def strip(side, rows, number):
         return pltpu.make_async_remote_copy(
             src_ref=strip_out.at[side, rows, :],
@@ -358,39 +355,83 @@
             device_id_type=MESH,
         )
 
-    def band(side):
+    def band(side, part):
         return pltpu.make_async_remote_copy(
-            src_ref=row_out.at[side],
-            dst_ref=row_in.at[side],
-            send_sem=fold_send.at[side, 3],
-            recv_sem=fold_recv.at[side, 3],
-            device_id=target[("up", "down")[side]],
+            src_ref=row_out.at[side, part],
+            dst_ref=row_in.at[side, part],
+            send_sem=fold_send.at[side, 3 + part],
+            recv_sem=fold_recv.at[side, 3 + part],
+            device_id=target[vertical[side]],
             device_id_type=MESH,
         )
 
+    def corner(side):
+        return pltpu.make_async_remote_copy(
+            src_ref=strip_out.at[jnp.where(odd, 1, 0), (low, high)[side], :],
+            dst_ref=corner_in.at[side],
+            send_sem=fold_send.at[side, 5],
+            recv_sem=fold_recv.at[side, 5],
+            device_id={**target[("up", "down")[side]], "ra": jnp.where(odd, ra + 1, ra - 1)},
+            device_id_type=MESH,
+        )
+
     pieces = ((low, 0), (high, 1), (mid, 2))
-    ways = ("left", "right")
+    ways, vertical = ("left", "right"), ("up", "down")
+    odd = ra % 2 == 1
+    even = jnp.logical_not(odd)
+    far = jnp.where(odd, exists["right"], exists["left"])
+
+    def sends(side, number):
+        return exists[ways[side]] & (True if number == 2 else (odd, even)[side])
+
+    def receives(side, number):
+        return exists[opposite[ways[side]]] & (True if number == 2 else (even, odd)[side])
     side_table = jnp.concatenate([table[:, low], table[:, high]], axis=1)
-
-    def send_strips(part, numbers):
-        values = dot(part, side_table)
-        start = 0
-        for number in numbers:
-            rows = pieces[number][0]
-            for side, cols in enumerate((low, high)):
-                block = values[start : start + rows.size, side * margin : (side + 1) * margin]
-                strip_out[side, rows, :] = (window[rows, cols] * block).astype(BF16)
-                @pl.when(exists[ways[side]])
-                def _(side=side, rows=rows, number=number):
-                    strip(side, rows, number).start()
-            start += rows.size
+    first = jnp.where(odd, 1, 0)
+
+    def put_strips(number, blocks):
+        rows = pieces[number][0]
+        for side, cols in enumerate((low, high)):
+            strip_out[side, rows, :] = (window[rows, cols] * blocks[side]).astype(BF16)
+
+            @pl.when(sends(side, number))
+            def _(side=side):
+                strip(side, rows, number).start()
 
     outer = inverse(outer_rows(lambda rows: turned[rows, :]))
-    send_strips(outer, (0, 1))
+    values = dot(outer, table[...])
+    for number, (rows, _) in enumerate(pieces[:2]):
+        block = values[number * margin : (number + 1) * margin]
+        put_strips(number, (block[:, :margin], block[:, margin + core :]))
+
+        @pl.when(exists[vertical[number]] & far)
+        def _(number=number):
+            corner(number).start()
+
+        for part, cols in enumerate((head, tail)):
+            inside = window[rows, cols] * block[:, margin * (1 + part) : margin * (2 + part)]
+            real[rows, cols] = inside
+            row_out[number, part] = inside.astype(BF16)
+
+        @pl.when(exists[vertical[number]])
+        def _(number=number):
+            band(number, first).start()
+
     middle = inverse(turned[mid, :])
-    send_strips(middle, (2,))
-    for part, (rows, number) in zip((outer[:margin], outer[margin:], middle), pieces):
-        synthesize(part, rows, mid)
+    values = dot(middle, side_table)
+    put_strips(2, (values[:, :margin], values[:, margin:]))
+    for number, (rows, _) in enumerate(pieces[:2]):
+        for side, part, cols in ((1, 0, head), (0, 1, tail)):
+            @pl.when(receives(side, number))
+            def _(side=side, part=part, cols=cols, rows=rows, number=number):
+                strip(side, rows, number).wait_recv()
+                row_out[number, part] = (real[rows, cols] + strip_in[side, rows, :].astype(F32)).astype(BF16)
+
+        @pl.when(exists[vertical[number]])
+        def _(number=number):
+            band(number, 1 - first).start()
+
+    real[mid, mid] = window[mid, mid] * dot(middle, table[:, mid])
 
     def drain(plane, carry):
         wait_send(plane, range(10))
@@ -398,36 +439,46 @@
 
     lax.fori_loop(0, PLANES, drain, 0)
 
-    def fold_columns(rows, number):
-        for side, cols in ((1, head), (0, tail)):
-            @pl.when(exists[opposite[ways[side]]])
-            def _(side=side, cols=cols):
-                strip(side, rows, number).wait_recv()
-                real[rows, cols] += strip_in[side, rows, :].astype(F32)
-
-    for side, (rows, number) in enumerate(pieces[:2]):
-        fold_columns(rows, number)
-        row_out[side] = real[rows, mid].astype(BF16)
-        @pl.when(exists[("up", "down")[side]])
+    for side, cols in ((1, head), (0, tail)):
+        @pl.when(receives(side, 2))
+        def _(side=side, cols=cols):
+            strip(side, mid, 2).wait_recv()
+            real[mid, cols] += strip_in[side, mid, :].astype(F32)
+
+    for side, rows in enumerate((tail, head)):
+        @pl.when(exists[opposite[vertical[side]]] & far)
         def _(side=side):
-            band(side).start()
-    fold_columns(*pieces[2])
-    for side, rows in ((1, head), (0, tail)):
-        @pl.when(exists[("down", "up")[side]])
+            corner(side).wait_recv()
+
+        for here, cols in ((even, head), (odd, tail)):
+            @pl.when(exists[opposite[vertical[side]]] & far & here)
+            def _(side=side, rows=rows, cols=cols):
+                real[rows, cols] += corner_in[side].astype(F32)
+
+    for side, rows in enumerate((tail, head)):
+        @pl.when(exists[opposite[vertical[side]]])
         def _(side=side, rows=rows):
-            band(side).wait_recv()
-            real[rows, mid] += row_in[side].astype(F32)
+            for part in range(2):
+                band(side, part).wait_recv()
+            for part, cols in enumerate((head, tail)):
+                real[rows, cols] += row_in[side, part].astype(F32)
+
     out_ref[...] = real[mid, mid]
 
     for side in range(2):
-        @pl.when(exists[ways[side]])
+        for rows, number in pieces:
+            @pl.when(sends(side, number))
+            def _(side=side, rows=rows, number=number):
+                strip(side, rows, number).wait_send()
+
+        @pl.when(exists[vertical[side]])
         def _(side=side):
-            for rows, number in pieces:
-                strip(side, rows, number).wait_send()
-
-        @pl.when(exists[("up", "down")[side]])
+            for part in range(2):
+                band(side, part).wait_send()
+
+        @pl.when(exists[vertical[side]] & far)
         def _(side=side):
-            band(side).wait_send()
+            corner(side).wait_send()
 
 
 def shards(n_dec, n_ra, constants, split_maps, white_noise):
@@ -468,13 +519,14 @@
             pltpu.VMEM((length, length), F32),
             pltpu.VMEM((2, length, margin), BF16),
             pltpu.VMEM((2, length, margin), BF16),
-            pltpu.VMEM((2, margin, core), BF16),
-            pltpu.VMEM((2, margin, core), BF16),
+            pltpu.VMEM((2, 2, margin, margin), BF16),
+            pltpu.VMEM((2, 2, margin, margin), BF16),
+            pltpu.VMEM((2, margin, margin), BF16),
             pltpu.SemaphoreType.DMA((13,)),
             pltpu.SemaphoreType.DMA((PLANES, 10)),
             pltpu.SemaphoreType.DMA((PLANES, 10)),
-            pltpu.SemaphoreType.DMA((2, 4)),
-            pltpu.SemaphoreType.DMA((2, 4)),
+            pltpu.SemaphoreType.DMA((2, 6)),
+            pltpu.SemaphoreType.DMA((2, 6)),
         ],
         compiler_params=pltpu.CompilerParams(
             collective_id=0, has_side_effects=True, vmem_limit_bytes=56 << 20

time: 31.1 us -> 30.9 us (level); the launches traced: 30.6 us -> 30.8 us
  no operation moved by 1% of the time
where the time goes in v3:
time: 30.9 us; the launch traced here: 30.8 us
  Pallas kernels  30.1 us (97%)
  other arithmetic  0.72 us (2%)
    pallas_call x1, Pallas kernels, shards(): pl.pallas_call(functools.partial(kernel, n_dec, n_ra, scale ** 0.5), out_...  30.1 us
    mul x1, other arithmetic, shards(): return result * (1.0 / (length * length))  0.72 us

profile of v3, /device:TPU:0, one launch (start us, length us, event | category | flops | bytes accessed | tf_op | source)
XLA Modules:
  0.0 30.8 jit_solution(2038078106565777666)
XLA Ops:
  0.0 30.1 %shard_map.100 = f32[256,256]{1,0:T(8,128)S(1)} custom-call(bf16[6,256,256]{2,1,0:T(8,128)(2,1)} %maps_hbm.1, bf16[512,512]{1,0:T(8,128)(2,1)} %noise_hbm.1, bf16[512,512]{1,0:T(8,128)(2,1)} %constant.18.clone.table_hbm, bf16[512,512]{1,0:T(8,128)(2,1)} %constant.19.clone.turned_hbm, bf16[272,256]{1,0:T(8,128)(2,1)} %constant.20.clone.rows_hbm, ...), custom_call_target="tpu_custom_call" | custom-call | tf_op jit(solution)/shard_map/pallas_call | solution.py:494
  30.1 0.7 %broadcast_multiply_fusion = f32[256,256]{1,0:T(8,128)} fusion(f32[256,256]{1,0:T(8,128)S(1)} %shard_map.100), kind=kLoop, calls=%fused_computation | loop fusion | flops 65536 | bytes 524288 | tf_op jit(solution)/shard_map/mul | solution.py:540

commit v4 on v3

--- a/solution.py
+++ b/solution.py
@@ -177,7 +177,7 @@
     tall_ref, wide_ref,
     ext, window, power, edge_rows, edge_cols, spectrum, sums, edge, last, real,
     strip_out, strip_in, row_out, row_in, corner_in,
-    local_sem, send_sem, recv_sem, fold_send, fold_recv,
+    local_sem, send_sem, recv_sem, fold_send, fold_recv, diagonal_sem,
 ):
     dec, ra = lax.axis_index("dec"), lax.axis_index("ra")
     length = noise.shape[0]
@@ -192,6 +192,11 @@
         "left": {"ra": ra - 1}, "right": {"ra": ra + 1},
     }
     opposite = {"up": "down", "down": "up", "left": "right", "right": "left"}
+    odd = ra % 2 == 1
+    even = jnp.logical_not(odd)
+    first = jnp.where(odd, 1, 0)
+    far = jnp.where(odd, exists["right"], exists["left"])
+    across = {"ra": jnp.where(odd, ra + 1, ra - 1)}
 
     pairs = [
         pltpu.make_async_copy(maps_hbm.at[pl.ds(2 * i, 2)], maps.at[pl.ds(2 * i, 2)], local_sem.at[i])
@@ -233,21 +238,46 @@
             device_id_type=MESH,
         )
 
+    vertical = ("up", "down")
+
+    def leaves(plane, number):
+        way = moves[number][0]
+        if number < 6:
+            return exists[way]
+        return exists[way] & ((odd if way == "left" else even) | (plane < PLANES - 1))
+
+    def arrives(plane, number):
+        way = moves[number][0]
+        if number < 6:
+            return exists[opposite[way]]
+        source = exists["down" if number % 2 == 0 else "up"]
+        return exists[opposite[way]] & ((even if way == "left" else odd) | source | (plane < PLANES - 1))
+
+    def diagonal(side):
+        return pltpu.make_async_remote_copy(
+            src_ref=ext.at[PLANES - 1, 1 + first, (head, tail)[side], :],
+            dst_ref=ext.at[PLANES - 1, 3 - 3 * first, (high, low)[side], :],
+            send_sem=diagonal_sem.at[side],
+            recv_sem=recv_sem.at[PLANES - 1, 6 + 2 * first + side],
+            device_id={**target[vertical[side]], **across},
+            device_id_type=MESH,
+        )
+
     def start(plane, numbers):
         for number in numbers:
-            @pl.when(exists[moves[number][0]])
+            @pl.when(leaves(plane, number))
             def _(number=number):
                 move(plane, number).start()
 
     def wait_recv(plane, numbers):
         for number in numbers:
-            @pl.when(exists[opposite[moves[number][0]]])
+            @pl.when(arrives(plane, number))
             def _(number=number):
                 move(plane, number).wait_recv()
 
     def wait_send(plane, numbers):
         for number in numbers:
-            @pl.when(exists[moves[number][0]])
+            @pl.when(leaves(plane, number))
             def _(number=number):
                 move(plane, number).wait_send()
 
@@ -272,6 +302,12 @@
         def _(rows=rows, blocks=blocks):
             ext[:, blocks, rows, :] = jnp.zeros((PLANES, blocks.size, rows.size, margin), BF16)
 
+    for way, rows in (("up", low), ("down", high)):
+        for here, block in ((even, 0), (odd, 3)):
+            @pl.when(jnp.logical_not(exists[way]) & far & here)
+            def _(rows=rows, block=block):
+                ext[PLANES - 1, block, rows, :] = jnp.zeros((margin, margin), BF16)
+
     for load in loads:
         load.wait()
     window[...] = tall_ref[...] * wide_ref[...]
@@ -326,13 +362,21 @@
 
     forward_corners(0)
     forward_corners(1)
-
-    def step(plane, carry):
-        forward_corners(plane)
-        gather_power(plane - 2)
+    forward_corners(2)
+    gather_power(0)
+    for side in range(2):
+        @pl.when(exists[vertical[side]] & far)
+        def _(side=side):
+            diagonal(side).start()
+
+    forward_corners(3)
+
+    def catch_up(plane, carry):
+        gather_power(plane)
         return carry
 
-    lax.fori_loop(2, PLANES, step, 0)
+    lax.fori_loop(1, 3, catch_up, 0)
+    forward_corners(PLANES - 1)
     gather_power(PLANES - 2)
     gather_last(PLANES - 1)
 
@@ -371,15 +415,12 @@
             dst_ref=corner_in.at[side],
             send_sem=fold_send.at[side, 5],
             recv_sem=fold_recv.at[side, 5],
-            device_id={**target[("up", "down")[side]], "ra": jnp.where(odd, ra + 1, ra - 1)},
+            device_id={**target[vertical[side]], **across},
             device_id_type=MESH,
         )
 
     pieces = ((low, 0), (high, 1), (mid, 2))
-    ways, vertical = ("left", "right"), ("up", "down")
-    odd = ra % 2 == 1
-    even = jnp.logical_not(odd)
-    far = jnp.where(odd, exists["right"], exists["left"])
+    ways = ("left", "right")
 
     def sends(side, number):
         return exists[ways[side]] & (True if number == 2 else (odd, even)[side])
@@ -387,7 +428,6 @@
     def receives(side, number):
         return exists[opposite[ways[side]]] & (True if number == 2 else (even, odd)[side])
     side_table = jnp.concatenate([table[:, low], table[:, high]], axis=1)
-    first = jnp.where(odd, 1, 0)
 
     def put_strips(number, blocks):
         rows = pieces[number][0]
@@ -438,6 +478,11 @@
         return carry
 
     lax.fori_loop(0, PLANES, drain, 0)
+    for side in range(2):
+        @pl.when(exists[vertical[side]] & far)
+        def _(side=side):
+            diagonal(side).wait_send()
+
 
     for side, cols in ((1, head), (0, tail)):
         @pl.when(receives(side, 2))
@@ -527,6 +572,7 @@
             pltpu.SemaphoreType.DMA((PLANES, 10)),
             pltpu.SemaphoreType.DMA((2, 6)),
             pltpu.SemaphoreType.DMA((2, 6)),
+            pltpu.SemaphoreType.DMA((2,)),
         ],
         compiler_params=pltpu.CompilerParams(
             collective_id=0, has_side_effects=True, vmem_limit_bytes=56 << 20

time: 30.9 us -> 30.5 us (0.987)
  Pallas kernels: 30.1 us -> 29.5 us
    pallas_call x1, Pallas kernels: 30.1 us -> 29.5 us  [shards(): pl.pallas_call(functools.partial(kernel, n_dec, n_ra, scale ** 0.5), out_...]
where the time goes in v4:
time: 30.5 us; the launch traced here: 30.2 us
  Pallas kernels  29.5 us (97%)
  other arithmetic  0.72 us (2%)
    pallas_call x1, Pallas kernels, shards(): pl.pallas_call(functools.partial(kernel, n_dec, n_ra, scale ** 0.5), out_...  29.5 us
    mul x1, other arithmetic, shards(): return result * (1.0 / (length * length))  0.72 us

profile of v4, /device:TPU:0, one launch (start us, length us, event | category | flops | bytes accessed | tf_op | source)
XLA Modules:
  0.0 30.2 jit_solution(7179059958896444940)
XLA Ops:
  0.0 29.5 %shard_map.100 = f32[256,256]{1,0:T(8,128)S(1)} custom-call(bf16[6,256,256]{2,1,0:T(8,128)(2,1)} %maps_hbm.1, bf16[512,512]{1,0:T(8,128)(2,1)} %noise_hbm.1, bf16[512,512]{1,0:T(8,128)(2,1)} %constant.18.clone.table_hbm, bf16[512,512]{1,0:T(8,128)(2,1)} %constant.19.clone.turned_hbm, bf16[272,256]{1,0:T(8,128)(2,1)} %constant.20.clone.rows_hbm, ...), custom_call_target="tpu_custom_call" | custom-call | tf_op jit(solution)/shard_map/pallas_call | solution.py:539
  29.5 0.7 %broadcast_multiply_fusion = f32[256,256]{1,0:T(8,128)} fusion(f32[256,256]{1,0:T(8,128)S(1)} %shard_map.100), kind=kLoop, calls=%fused_computation | loop fusion | flops 65536 | bytes 524288 | tf_op jit(solution)/shard_map/mul | solution.py:586

commit v5 on v4

--- a/solution.py
+++ b/solution.py
@@ -27,7 +27,9 @@
         distance = np.abs(left[:, None] - right[None, :]) % length
         return (np.minimum(distance, length - distance) <= SMOOTH).astype(np.float64)
 
-    signed = np.concatenate([np.arange(half + 1), -np.arange(1, half)])
+    parity = np.concatenate([np.arange(0, half, 2), np.arange(1, half, 2)])
+    order = np.concatenate([parity, half + parity])
+    signed = np.concatenate([np.arange(half + 1), -np.arange(1, half)])[order]
     kept = np.arange(half + PAD)
     smooth_rows = near(kept, np.arange(half)) * (kept <= half)[:, None]
     first = np.arange(PAD)
@@ -38,7 +40,7 @@
     fold_last[:, PAD] = near(last, np.array([half]))[:, 0]
     fold_last[last > half] = 0.0
     return dict(
-        packed=packed, profile=profile, smooth_cols=near(signed, signed), smooth_rows=smooth_rows,
+        packed=packed, packed_cols=packed[order], profile=profile, smooth_cols=near(signed, signed), smooth_rows=smooth_rows,
         fold_first=fold_first, fold_last=fold_last, total=float(np.sum(profile**2) ** 2),
     )
 
@@ -170,12 +172,12 @@
 
 def kernel(
     n_dec, n_ra, factor,
-    maps_hbm, noise_hbm, table_hbm, turned_hbm, rows_hbm, cols_hbm, first_hbm, last_hbm,
+    maps_hbm, noise_hbm, table_hbm, turned_hbm, table_cols_hbm, turned_cols_hbm, rows_hbm, cols_hbm, first_hbm, last_hbm,
     tall_hbm, wide_hbm,
     out_ref,
-    maps, noise, table, turned, smooth_rows, smooth_cols, fold_first, fold_last,
+    maps, noise, table, turned, table_cols, turned_cols, smooth_rows, smooth_cols, fold_first, fold_last,
     tall_ref, wide_ref,
-    ext, window, power, edge_rows, edge_cols, spectrum, sums, edge, last, real,
+    ext, window, power, edge_rows, edge_cols, inner_part, outer_part, sums, edge, last, real,
     strip_out, strip_in, row_out, row_in, corner_in,
     local_sem, send_sem, recv_sem, fold_send, fold_recv, diagonal_sem,
 ):
@@ -206,8 +208,8 @@
         pltpu.make_async_copy(source, place, local_sem.at[3 + number])
         for number, (source, place) in enumerate(
             [(tall_hbm, tall_ref), (wide_hbm, wide_ref), (noise_hbm, noise), (table_hbm, table),
-             (turned_hbm, turned), (rows_hbm, smooth_rows), (cols_hbm, smooth_cols),
-             (first_hbm, fold_first), (last_hbm, fold_last)]
+             (turned_cols_hbm, turned_cols), (turned_hbm, turned), (table_cols_hbm, table_cols),
+             (rows_hbm, smooth_rows), (cols_hbm, smooth_cols), (first_hbm, fold_first), (last_hbm, fold_last)]
         )
     ]
     for load in pairs:
@@ -308,16 +310,22 @@
             def _(rows=rows, block=block):
                 ext[PLANES - 1, block, rows, :] = jnp.zeros((margin, margin), BF16)
 
-    for load in loads:
+    for load in loads[:5]:
         load.wait()
     window[...] = tall_ref[...] * wide_ref[...]
     for total in (power, edge_rows, edge_cols):
         total[...] = jnp.zeros_like(total)
 
-    def transform(tile):
-        return dot(dot(table[...], tile).astype(BF16), turned[...])
-
-    combine(transform(noise[...]), factor, sums, edge, last)
+    combine(
+        dot(dot(table[...], noise[...]).astype(BF16), turned_cols[...]), factor, sums, edge, last
+    )
+
+    def spectra(left, right):
+        even_cols = jnp.concatenate([turned_cols[:half, :margin], turned_cols[:half, half : half + margin]], axis=1)
+        odd_cols = jnp.concatenate([turned_cols[:half, margin:half], turned_cols[:half, half + margin :]], axis=1)
+        evens = dot((left + right).astype(BF16), even_cols)
+        odds = dot((left - right).astype(BF16), odd_cols)
+        return jnp.concatenate([evens[:, :margin], odds[:, :margin], evens[:, margin:], odds[:, margin:]], axis=1)
 
     def forward_corners(plane):
         for number in (0, 3, 2, 1):
@@ -333,21 +341,25 @@
 
     def gather_power(plane):
         wait_recv(plane, range(4, 10))
-        add_power(transform(windowed(plane, whole, range(4))))
+        halves = dot(table[...], windowed(plane, whole, range(4)))
+        add_power(spectra(halves[:, :half], halves[:, half:]))
 
     def outer_rows(values):
         return jnp.concatenate([values(low), values(high)], axis=0)
 
-    def gather_last(plane):
-        halves = dot(table[...], windowed(plane, whole, (1, 2))).astype(BF16)
-        spectrum[...] = dot(halves, turned[mid, :])
+    def gather_inner(plane, slot):
+        inner_part[slot] = dot(table[...], windowed(plane, whole, (1, 2)))
         wait_recv(plane, (4, 5))
-        sides = dot(table[:, mid], windowed(plane, mid, (0, 3)))
+        outer_part[slot] = dot(table[:, mid], windowed(plane, mid, (0, 3)))
+
+    def gather_outer(plane, slot):
         wait_recv(plane, range(6, 10))
         corners = outer_rows(lambda rows: windowed(plane, rows, (0, 3)))
         outer_table = jnp.concatenate([table[:, low], table[:, high]], axis=1)
-        sides = (sides + dot(outer_table, corners)).astype(BF16)
-        add_power(spectrum[...] + dot(sides, outer_rows(lambda rows: turned[rows, :])))
+        sides = outer_part[slot] + dot(outer_table, corners)
+        left = jnp.concatenate([sides[:, :margin], inner_part[slot, :, :margin]], axis=1)
+        right = jnp.concatenate([inner_part[slot, :, margin:], sides[:, margin:]], axis=1)
+        add_power(spectra(left, right))
 
     def add_power(values):
         a, b = values[:half, :half], values[:half, half:]
@@ -375,10 +387,15 @@
         gather_power(plane)
         return carry
 
-    lax.fori_loop(1, 3, catch_up, 0)
+    lax.fori_loop(1, 2, catch_up, 0)
+    gather_inner(PLANES - 2, 0)
     forward_corners(PLANES - 1)
-    gather_power(PLANES - 2)
-    gather_last(PLANES - 1)
+    gather_power(2)
+    gather_inner(PLANES - 1, 1)
+    for load in loads[5:]:
+        load.wait()
+    gather_outer(PLANES - 2, 0)
+    gather_outer(PLANES - 1, 1)
 
     gain = gains(
         power[...], edge_rows[...], edge_cols[...], smooth_rows[...], smooth_cols[...],
@@ -427,7 +444,7 @@
 
     def receives(side, number):
         return exists[opposite[ways[side]]] & (True if number == 2 else (even, odd)[side])
-    side_table = jnp.concatenate([table[:, low], table[:, high]], axis=1)
+    side_table = jnp.concatenate([table_cols[:, low], table_cols[:, high]], axis=1)
 
     def put_strips(number, blocks):
         rows = pieces[number][0]
@@ -439,7 +456,7 @@
                 strip(side, rows, number).start()
 
     outer = inverse(outer_rows(lambda rows: turned[rows, :]))
-    values = dot(outer, table[...])
+    values = dot(outer, table_cols[...])
     for number, (rows, _) in enumerate(pieces[:2]):
         block = values[number * margin : (number + 1) * margin]
         put_strips(number, (block[:, :margin], block[:, margin + core :]))
@@ -471,7 +488,7 @@
         def _(number=number):
             band(number, 1 - first).start()
 
-    real[mid, mid] = window[mid, mid] * dot(middle, table[:, mid])
+    real[mid, mid] = window[mid, mid] * dot(middle, table_cols[:, mid])
 
     def drain(plane, carry):
         wait_send(plane, range(10))
@@ -533,16 +550,20 @@
     as_f32 = lambda values: jnp.asarray(np.asarray(values, np.float32))
     packed = as_bf16(constants["packed"])
     turned = as_bf16(constants["packed"].T)
+    table_cols = as_bf16(constants["packed_cols"])
+    turned_cols = as_bf16(constants["packed_cols"].T)
     scale = WEIGHT / ((splits - 1) * constants["total"] * (2 * SMOOTH + 1) ** 2)
     in_vmem = pl.BlockSpec(memory_space=pltpu.VMEM)
     in_hbm = pl.BlockSpec(memory_space=pl.ANY)
     result = pl.pallas_call(
         functools.partial(kernel, n_dec, n_ra, scale**0.5),
         out_shape=pltpu.VMEM((core, core), F32),
-        in_specs=[in_hbm] * 10,
+        in_specs=[in_hbm] * 12,
         out_specs=in_vmem,
         scratch_shapes=[
             pltpu.VMEM((splits, core, core), BF16),
+            pltpu.VMEM((length, length), BF16),
+            pltpu.VMEM((length, length), BF16),
             pltpu.VMEM((length, length), BF16),
             pltpu.VMEM((length, length), BF16),
             pltpu.VMEM((length, length), BF16),
@@ -557,7 +578,8 @@
             pltpu.VMEM((half, length), F32),
             pltpu.VMEM((PAD, length), F32),
             pltpu.VMEM((half, 256), F32),
-            pltpu.VMEM((length, length), F32),
+            pltpu.VMEM((2, length, half), F32),
+            pltpu.VMEM((2, length, half), F32),
             pltpu.VMEM((4, half, half), F32),
             pltpu.VMEM((2, half, 128), F32),
             pltpu.VMEM((8, length), F32),
@@ -567,7 +589,7 @@
             pltpu.VMEM((2, 2, margin, margin), BF16),
             pltpu.VMEM((2, 2, margin, margin), BF16),
             pltpu.VMEM((2, margin, margin), BF16),
-            pltpu.SemaphoreType.DMA((13,)),
+            pltpu.SemaphoreType.DMA((14,)),
             pltpu.SemaphoreType.DMA((PLANES, 10)),
             pltpu.SemaphoreType.DMA((PLANES, 10)),
             pltpu.SemaphoreType.DMA((2, 6)),
@@ -578,7 +600,7 @@
             collective_id=0, has_side_effects=True, vmem_limit_bytes=56 << 20
         ),
     )(
-        split_maps, white_noise, packed, turned,
+        split_maps, white_noise, packed, turned, table_cols, turned_cols,
         as_bf16(constants["smooth_rows"]), as_bf16(constants["smooth_cols"]),
         as_bf16(constants["fold_first"]), as_bf16(constants["fold_last"]),
         as_f32(constants["profile"][:, None]), as_f32(constants["profile"][None, :]),

time: 30.5 us -> 29.7 us (0.974)
  Pallas kernels: 29.5 us -> 28.8 us
    pallas_call x1, Pallas kernels: 29.5 us -> 28.8 us  [shards(): pl.pallas_call(functools.partial(kernel, n_dec, n_ra, scale ** 0.5), out_...]
where the time goes in v5:
time: 29.7 us; the launch traced here: 29.5 us
  Pallas kernels  28.8 us (97%)
  other arithmetic  0.72 us (2%)
    pallas_call x1, Pallas kernels, shards(): pl.pallas_call(functools.partial(kernel, n_dec, n_ra, scale ** 0.5), out_...  28.8 us
    mul x1, other arithmetic, shards(): return result * (1.0 / (length * length))  0.72 us

profile of v5, /device:TPU:0, one launch (start us, length us, event | category | flops | bytes accessed | tf_op | source)
XLA Modules:
  0.0 29.5 jit_solution(3915327804403488126)
XLA Ops:
  0.0 28.8 %shard_map.118 = f32[256,256]{1,0:T(8,128)S(1)} custom-call(bf16[6,256,256]{2,1,0:T(8,128)(2,1)} %maps_hbm.1, bf16[512,512]{1,0:T(8,128)(2,1)} %noise_hbm.1, bf16[512,512]{1,0:T(8,128)(2,1)} %constant.22.clone.table_hbm, bf16[512,512]{1,0:T(8,128)(2,1)} %constant.23.clone.turned_hbm, bf16[512,512]{1,0:T(8,128)(2,1)} %constant.24.clone.table_cols_hbm, ...), custom_call_target="tpu_custom_call" | custom-call | tf_op jit(solution)/shard_map/pallas_call | solution.py:558
  28.8 0.7 %broadcast_multiply_fusion = f32[256,256]{1,0:T(8,128)} fusion(f32[256,256]{1,0:T(8,128)S(1)} %shard_map.118), kind=kLoop, calls=%fused_computation | loop fusion | flops 65536 | bytes 524288 | tf_op jit(solution)/shard_map/mul | solution.py:608

commit v6 on v5

--- a/solution.py
+++ b/solution.py
@@ -474,9 +474,6 @@
         def _(number=number):
             band(number, first).start()
 
-    middle = inverse(turned[mid, :])
-    values = dot(middle, side_table)
-    put_strips(2, (values[:, :margin], values[:, margin:]))
     for number, (rows, _) in enumerate(pieces[:2]):
         for side, part, cols in ((1, 0, head), (0, 1, tail)):
             @pl.when(receives(side, number))
@@ -488,6 +485,9 @@
         def _(number=number):
             band(number, 1 - first).start()
 
+    middle = inverse(turned[mid, :])
+    values = dot(middle, side_table)
+    put_strips(2, (values[:, :margin], values[:, margin:]))
     real[mid, mid] = window[mid, mid] * dot(middle, table_cols[:, mid])
 
     def drain(plane, carry):

time: 29.7 us -> 29.6 us (level)
  no operation moved by 1% of the time
where the time goes in v6:
time: 29.6 us; the launch traced here: 29.5 us
  Pallas kernels  28.7 us (97%)
  other arithmetic  0.72 us (2%)
    pallas_call x1, Pallas kernels, shards(): pl.pallas_call(functools.partial(kernel, n_dec, n_ra, scale ** 0.5), out_...  28.7 us
    mul x1, other arithmetic, shards(): return result * (1.0 / (length * length))  0.72 us

profile of v6, /device:TPU:0, one launch (start us, length us, event | category | flops | bytes accessed | tf_op | source)
XLA Modules:
  0.0 29.5 jit_solution(535364853091871019)
XLA Ops:
  0.0 28.7 %shard_map.118 = f32[256,256]{1,0:T(8,128)S(1)} custom-call(bf16[6,256,256]{2,1,0:T(8,128)(2,1)} %maps_hbm.1, bf16[512,512]{1,0:T(8,128)(2,1)} %noise_hbm.1, bf16[512,512]{1,0:T(8,128)(2,1)} %constant.22.clone.table_hbm, bf16[512,512]{1,0:T(8,128)(2,1)} %constant.23.clone.turned_hbm, bf16[512,512]{1,0:T(8,128)(2,1)} %constant.24.clone.table_cols_hbm, ...), custom_call_target="tpu_custom_call" | custom-call | tf_op jit(solution)/shard_map/pallas_call | solution.py:558
  28.7 0.7 %broadcast_multiply_fusion = f32[256,256]{1,0:T(8,128)} fusion(f32[256,256]{1,0:T(8,128)S(1)} %shard_map.118), kind=kLoop, calls=%fused_computation | loop fusion | flops 65536 | bytes 524288 | tf_op jit(solution)/shard_map/mul | solution.py:608

commit v7 on v6

--- a/solution.py
+++ b/solution.py
@@ -241,6 +241,7 @@
         )
 
     vertical = ("up", "down")
+    near_first = (((0, 1), odd), ((2, 3), even), ((0, 1), even), ((2, 3), odd))
 
     def leaves(plane, number):
         way = moves[number][0]
@@ -265,15 +266,15 @@
             device_id_type=MESH,
         )
 
-    def start(plane, numbers):
+    def start(plane, numbers, here=True):
         for number in numbers:
-            @pl.when(leaves(plane, number))
+            @pl.when(leaves(plane, number) & here)
             def _(number=number):
                 move(plane, number).start()
 
-    def wait_recv(plane, numbers):
+    def wait_recv(plane, numbers, here=True):
         for number in numbers:
-            @pl.when(arrives(plane, number))
+            @pl.when(arrives(plane, number) & here)
             def _(number=number):
                 move(plane, number).wait_recv()
 
@@ -292,7 +293,12 @@
         ext[plane, 2, mid, :] = values[:, margin:]
         if plane == 0:
             pl.semaphore_wait(barrier, sum(here.astype(jnp.int32) for here in exists.values()))
-        start(plane, (0, 3, 2, 1, 4, 5))
+        if plane < PLANES - 1:
+            start(plane, (0, 3, 2, 1, 4, 5))
+        else:
+            for numbers, here in near_first:
+                start(plane, numbers, here)
+            start(plane, (4, 5))
 
     for load in loads:
         load.start()
@@ -389,7 +395,10 @@
 
     lax.fori_loop(1, 2, catch_up, 0)
     gather_inner(PLANES - 2, 0)
-    forward_corners(PLANES - 1)
+    for numbers, here in near_first:
+        for number in numbers:
+            wait_recv(PLANES - 1, (number,), here)
+            start(PLANES - 1, (6 + number,), here)
     gather_power(2)
     gather_inner(PLANES - 1, 1)
     for load in loads[5:]:

time: 29.6 us -> 29.7 us (level)
  no operation moved by 1% of the time
where the time goes in v7:
time: 29.7 us; the launch traced here: 29.5 us
  Pallas kernels  28.7 us (97%)
  other arithmetic  0.72 us (2%)
    pallas_call x1, Pallas kernels, shards(): pl.pallas_call(functools.partial(kernel, n_dec, n_ra, scale ** 0.5), out_...  28.7 us
    mul x1, other arithmetic, shards(): return result * (1.0 / (length * length))  0.72 us

profile of v7, /device:TPU:0, one launch (start us, length us, event | category | flops | bytes accessed | tf_op | source)
XLA Modules:
  0.0 29.5 jit_solution(16577642673320111570)
XLA Ops:
  0.0 28.7 %shard_map.118 = f32[256,256]{1,0:T(8,128)S(1)} custom-call(bf16[6,256,256]{2,1,0:T(8,128)(2,1)} %maps_hbm.1, bf16[512,512]{1,0:T(8,128)(2,1)} %noise_hbm.1, bf16[512,512]{1,0:T(8,128)(2,1)} %constant.22.clone.table_hbm, bf16[512,512]{1,0:T(8,128)(2,1)} %constant.23.clone.turned_hbm, bf16[512,512]{1,0:T(8,128)(2,1)} %constant.24.clone.table_cols_hbm, ...), custom_call_target="tpu_custom_call" | custom-call | tf_op jit(solution)/shard_map/pallas_call | solution.py:567
  28.8 0.7 %broadcast_multiply_fusion = f32[256,256]{1,0:T(8,128)} fusion(f32[256,256]{1,0:T(8,128)S(1)} %shard_map.118), kind=kLoop, calls=%fused_computation | loop fusion | flops 65536 | bytes 524288 | tf_op jit(solution)/shard_map/mul | solution.py:617
